TPU v7x, 512 devices: a whole 4x8x8 slice. The times are simulated.
512 devices in a mesh: band: 4 (over x), ty: 16 (over y, core), tx: 8 (over z).
Axes of the slice: x: 4, y: 8, z: 8, core: 2. Of those that a mesh axis runs over, the one named last changes fastest.
Arguments:
- dirty: float32 [8, 4096, 2048], P('band', 'ty', 'tx'), may hold values from -6 to 6
- psf: bfloat16 [8, 20, 2304], P('band'), may hold values from -4 to 4
- comp_tile: int32 [16384, 1], P(('ty', 'tx')), may hold values from 0 to 127; in each aligned block of 128 rows (0 to 127, 128 to 255, ...) at most 2 rows name the same one
- comp_offset: int32 [16384, 2], P(('ty', 'tx')), may hold values from 0 to 255
- comp_scale: int32 [16384], P(('ty', 'tx')), may hold values from 0 to 4
- comp_amp: float32 [16384, 4], P(('ty', 'tx')), may hold values from -6 to 6
- fit_weight: float32 [8, 4], P('band'), may hold values from -5 to 5
Outputs:
- residual: float32 [8, 4096, 2048], P('band', 'ty', 'tx')
- taylor_fit: float32 [4, 4096, 2048], P('band', 'ty', 'tx')
Inputs may be any that keep to these rules, and one draw needn't show every extreme that they name: `comp_tile`: the 128 components of one device name at most 2 components for one tile, and exactly 2 for some tile on some device.
All inputs are finite; a program needn't handle non-finite values.
Results may differ from a plain program's by a relative error of at most 0.0022.
Values may be sent and summed in bfloat16 or wider, within the bound.
A program may use at most 64 MiB of HBM per device.

v0:
```python
import functools

import jax
import jax.numpy as jnp
from jax import lax
from jax.experimental import pallas as pl
from jax.experimental.pallas import tpu as pltpu
from jax.sharding import PartitionSpec as P

TAYLOR = 4
SCALES = 5
PATCH = 48
ROWS_K = TAYLOR * SCALES
PAD_K = 24
HALF = PATCH // 2
WIDE = HALF * PATCH
SIDE = 256
SLOTS = 8
WORDS = 8
ROW_BASE = 48
COL_BASE = 64
BLOCKS = 6
CANVAS = 352
GROUPS = (48, 16, 8)
OUT_ROWS = 64
MESH = pl.DeviceIdType.MESH


def sends_of_tiles(tile, off, scale, amp, n_ty, n_tx):
    count = tile.shape[1]
    tiles = n_ty * n_tx
    comp_y = lax.shift_right_logical(tile, n_tx.bit_length() - 1)
    comp_x = lax.bitwise_and(tile, n_tx - 1)
    over_r = (off[0:1] + PATCH > SIDE).astype(jnp.int32)
    over_c = (off[1:2] + PATCH > SIDE).astype(jnp.int32)
    dest = lax.broadcasted_iota(jnp.int32, (tiles, count), 0)
    half = tiles // 2
    bits = n_tx.bit_length() - 1
    core = lax.shift_right_logical(dest, half.bit_length() - 1)
    inner = lax.bitwise_and(dest, half - 1)
    dest_x = lax.bitwise_and(inner, n_tx - 1)
    dest_y = 2 * lax.shift_right_logical(inner, bits) + core
    down, right = dest_y - comp_y, dest_x - comp_x
    touches = ((down == 0) | ((down == 1) & (over_r == 1))) & (
        (right == 0) | ((right == 1) & (over_c == 1))
    )
    before = (
        lax.broadcasted_iota(jnp.int32, (count, count), 0)
        < lax.broadcasted_iota(jnp.int32, (count, count), 1)
    ).astype(jnp.float32)
    rank = jnp.dot(
        jnp.where(touches, 1.0, 0.0).astype(jnp.bfloat16),
        before.astype(jnp.bfloat16),
        preferred_element_type=jnp.float32,
    )
    rank = jnp.where(touches, rank, -1.0)
    chosen = jnp.concatenate(
        [jnp.where(rank == float(k), 1.0, 0.0).astype(jnp.bfloat16) for k in range(SLOTS)], axis=1
    )
    rows = (comp_y * SIDE + off[0:1]).astype(jnp.float32)
    cols = (comp_x * SIDE + off[1:2]).astype(jnp.float32)
    record = jnp.concatenate(
        [rows, cols, scale.astype(jnp.float32), jnp.ones((1, count), jnp.float32), amp], axis=0
    )
    high = record.astype(jnp.bfloat16).astype(jnp.float32)
    rest = record - high
    middle = rest.astype(jnp.bfloat16).astype(jnp.float32)
    low = rest - middle
    place = lax.shift_right_logical(
        lax.broadcasted_iota(jnp.int32, (SLOTS * WORDS, count), 0), 3
    )
    parts = []
    for part in (high, middle, low):
        tall = jnp.concatenate([part] * SLOTS, axis=0)
        parts.append(
            jnp.concatenate([jnp.where(place == k, tall, 0.0) for k in range(SLOTS)], axis=1)
        )
    parts.append(jnp.zeros_like(parts[0]))
    table = jnp.concatenate(parts, axis=0).astype(jnp.bfloat16)
    found = lax.dot_general(
        chosen, table, (((1,), (1,)), ((), ())), preferred_element_type=jnp.float32
    )
    found = found[:, :128] + found[:, 128:]
    found = found + pltpu.roll(found, 64, 1)
    lane = lax.broadcasted_iota(jnp.int32, (half, 128), 1)
    return jnp.where(lane < 64, found[:half], found[half:])


def unrolled(first, last, lane, step):
    tile, shift = divmod(step * PATCH, 128)
    out = []
    for table, base in ((first, 0), (last, 64)):
        value = table(tile)
        if shift + PATCH > 128:
            value = jnp.where(lane >= shift, value, table(tile + 1))
        turn = (base - shift) % 128
        out.append(pltpu.roll(value, turn, 1) if turn else value)
    return jnp.where(
        lane < PATCH, out[0], jnp.where((lane >= 64) & (lane < 64 + PATCH), out[1], 0.0)
    )


def exchange_kernel(
    n_band, n_ty, n_tx,
    tile_hbm, off_hbm, scale_hbm, amp_hbm, weight_hbm, dirty_hbm, psf_hbm,
    value_ref, list_ref, table_ref, taylor_table_ref, fit_ref,
    tile_ref, off_ref, scale_ref, amp_ref, weight_ref, dirty_ref, psf_ref,
    send, cross, got, psf, fit_send, fit_got, tab_send, tab_own, tab_got,
    x_send, x_recv, y_send, y_recv, b_send, b_recv, own_sem, pair_send, pair_recv, load_sem,
):
    me_b, me_y, me_x = lax.axis_index("band"), lax.axis_index("ty"), lax.axis_index("tx")
    barrier = pltpu.get_barrier_semaphore()
    along_x = [lax.rem(me_x + o, n_tx) for o in range(1, n_tx)]
    along_y = [lax.rem(me_y + o, n_ty) for o in range(1, n_ty)]
    along_b = [lax.rem(me_b + o, n_band) for o in range(1, n_band)]
    partners = (
        [(me_b, me_y, x) for x in along_x]
        + [(me_b, y, me_x) for y in along_y]
        + [(b, me_y, me_x) for b in along_b]
    )
    for partner in partners:
        pl.semaphore_signal(barrier, inc=1, device_id=partner, device_id_type=MESH)

    loads = [
        pltpu.make_async_copy(source, target, load_sem.at[i])
        for i, (source, target) in enumerate((
            (tile_hbm, tile_ref), (off_hbm, off_ref), (scale_hbm, scale_ref), (amp_hbm, amp_ref),
            (weight_hbm, weight_ref), (psf_hbm, psf_ref), (dirty_hbm, dirty_ref),
        ))
    ]
    for load in loads:
        load.start()

    for load in loads[:4]:
        load.wait()
    records = sends_of_tiles(tile_ref[...], off_ref[...], scale_ref[...], amp_ref[...], n_ty, n_tx)
    for y in range(n_ty // 2):
        send[y] = records[y * n_tx:(y + 1) * n_tx]

    pl.semaphore_wait(barrier, len(partners))

    def in_all(ref, send_sem, recv_sem, partner):
        return pltpu.make_async_remote_copy(
            src_ref=ref, dst_ref=ref, send_sem=send_sem.at[0], recv_sem=recv_sem.at[0],
            device_id=partner, device_id_type=MESH,
        )

    for y in along_y:
        copy = pltpu.make_async_remote_copy(
            src_ref=send.at[y // 2], dst_ref=cross.at[me_y],
            send_sem=y_send.at[0], recv_sem=y_recv.at[0],
            device_id=(me_b, y, me_x), device_id_type=MESH,
        )
        copy.start()
    stage_y = in_all(cross.at[pl.ds(0, n_ty - 1)], y_send, y_recv, partners[-n_band])
    own = pltpu.make_async_copy(send.at[me_y // 2], cross.at[me_y], own_sem.at[0])
    own.start()
    for load in loads[4:]:
        load.wait()
    for b in range(2):
        psf[b, 0:ROWS_K, :] = psf_ref[:, b, :].astype(jnp.float32)
        psf[b, ROWS_K:PAD_K, :] = jnp.zeros((PAD_K - ROWS_K, 2 * WIDE), jnp.float32)
    core = lax.rem(me_y, 2)
    mine = [
        jnp.where(core == 1, psf[b, :, WIDE:2 * WIDE], psf[b, :, 0:WIDE]) for b in range(2)
    ]
    for o in range(1, n_band):
        w0, w1 = weight_ref[0, along_b[o - 1]], weight_ref[1, along_b[o - 1]]
        tab_send[o - 1] = w0 * mine[0] + w1 * mine[1]
        fit_send[o - 1] = (w0 * dirty_ref[0] + w1 * dirty_ref[1]).astype(jnp.bfloat16)

    w0, w1 = weight_ref[0, me_b], weight_ref[1, me_b]
    tab_own[core] = w0 * mine[0] + w1 * mine[1]
    lane24 = lax.broadcasted_iota(jnp.int32, (PAD_K, 128), 1)

    def piece(ref, half):
        return lambda t: ref[:, half * WIDE + t * 128:half * WIDE + (t + 1) * 128]

    def band_table(half):
        first, last = piece(psf.at[0], half), piece(psf.at[1], half)
        for step in range(HALF):
            table_ref[pl.ds(half * HALF + step, PAD_K, stride=PATCH), :] = unrolled(
                first, last, lane24, step
            )

    band_table(0)

    stage_t, stage_f = [], []
    for source, target, which, copies in (
        (tab_send, tab_got, 0, stage_t), (fit_send, fit_got, 1, stage_f)
    ):
        for o, b in enumerate(along_b):
            copy = pltpu.make_async_remote_copy(
                src_ref=source.at[o], dst_ref=target.at[o],
                send_sem=b_send.at[which, o], recv_sem=b_recv.at[which, o],
                device_id=(b, me_y, me_x), device_id_type=MESH,
            )
            copy.start()
            copies.append(copy)

    own.wait()
    stage_y.wait_recv()
    for x in along_x:
        copy = pltpu.make_async_remote_copy(
            src_ref=cross.at[:, x, :], dst_ref=got.at[:, me_x, :],
            send_sem=x_send.at[0], recv_sem=x_recv.at[0],
            device_id=(me_b, me_y, x), device_id_type=MESH,
        )
        copy.start()
    stage_x = in_all(got.at[:, pl.ds(0, n_tx - 1), :], x_send, x_recv, partners[0])
    own = pltpu.make_async_copy(cross.at[:, me_x, :], got.at[:, me_x, :], own_sem.at[1])
    own.start()

    for copy in stage_t:
        copy.wait_recv()
    for o in range(n_band - 1):
        tab_own[core] += tab_got[o]
    band_table(1)
    pair = pltpu.make_async_remote_copy(
        src_ref=tab_own.at[core], dst_ref=tab_own.at[core],
        send_sem=pair_send.at[0], recv_sem=pair_recv.at[0],
        device_id=(me_b, me_y + 1 - 2 * core, me_x), device_id_type=MESH,
    )
    pair.start()

    pair.wait_recv()
    first, last = piece(tab_own.at[0], 0), piece(tab_own.at[1], 0)
    for step in range(HALF):
        taylor_table_ref[pl.ds(step, PAD_K, stride=HALF), :] = unrolled(first, last, lane24, step)

    fit_ref[...] = w0 * dirty_ref[0] + w1 * dirty_ref[1]
    for copy in stage_f:
        copy.wait_recv()
    for o in range(n_band - 1):
        fit_ref[...] += fit_got[o].astype(jnp.float32)
    own.wait()
    stage_x.wait_recv()
    sources = n_ty * n_tx
    slots = jnp.concatenate([got[y] for y in range(n_ty)], axis=0)
    slots = jnp.where(lax.rem(me_y, 2) == 1, pltpu.roll(slots, 64, 1), slots)
    lane = lax.broadcasted_iota(jnp.int32, (sources, 128), 1)
    word = lax.bitwise_and(lane, WORDS - 1)
    move_r = (ROW_BASE - me_y * SIDE).astype(jnp.float32)
    move_c = (COL_BASE - me_x * SIDE).astype(jnp.float32)
    row = jnp.clip(slots + move_r, 0.0, float(ROW_BASE + SIDE)).astype(jnp.int32)
    col = jnp.clip(
        pltpu.roll(slots, 127, 1) + move_c, 0.0, float(COL_BASE + SIDE)
    ).astype(jnp.int32)
    scale = jnp.clip(pltpu.roll(slots, 126, 1), 0.0, float(SCALES)).astype(jnp.int32)
    place = row + lax.shift_right_logical(col, 6) * CANVAS
    place = place + lax.shift_left(lax.bitwise_and(col, 63), 11) + lax.shift_left(scale, 17)
    value = jnp.where(word == 0, place.astype(jnp.float32), slots)
    quarter = sources // 4
    part = lax.shift_right_logical(lax.broadcasted_iota(jnp.int32, (quarter, 128), 1), 5)
    for first, turn in ((0, 0), (quarter + 8, 96)):
        packed = jnp.zeros((quarter, 128), jnp.float32)
        for q in range(4):
            own_rows = value[q * quarter:(q + 1) * quarter]
            moved = (q * 32 + turn) % 128
            packed = jnp.where(part == q, pltpu.roll(own_rows, moved, 1) if moved else own_rows, packed)
        value_ref[first:first + quarter] = packed
    used = jnp.sum(
        jnp.where((word == 3) & (lane < 64), slots, 0.0), axis=1, keepdims=True
    )
    used = jnp.broadcast_to(used, (sources, 128))
    earlier = (
        lax.broadcasted_iota(jnp.int32, (sources, sources), 1)
        < lax.broadcasted_iota(jnp.int32, (sources, sources), 0)
    ).astype(jnp.float32).astype(jnp.bfloat16)
    start = jnp.dot(earlier, used.astype(jnp.bfloat16), preferred_element_type=jnp.float32)
    end = start + used
    lists = max(1, sources * SLOTS // 128)
    for i in range(lists):
        order = (lane + i * 128).astype(jnp.float32)
        source = jnp.sum(jnp.where(end <= order, 1.0, 0.0), axis=0, keepdims=True)
        base = jnp.max(jnp.where(start <= order, start, 0.0), axis=0, keepdims=True)
        group = sum(jnp.where(source >= float(q * quarter), 1.0, 0.0) for q in (1, 2, 3))
        slot = order[0:1] - base
        far = jnp.where(slot >= 4.0, 1.0, 0.0)
        index = (source - group * quarter + far * (quarter + 8)) * 128.0 + group * 32.0
        index = index + (slot - 4.0 * far) * WORDS
        index = jnp.where(source < float(sources), index, float(quarter * 128))
        list_ref[i:i + 1, :] = index.astype(jnp.int32)
    spot = lax.broadcasted_iota(jnp.int32, (8, 128), 1)
    count = end[sources - 1:sources]
    most = jnp.max(used, axis=0, keepdims=True)
    value_ref[quarter:quarter + 8] = jnp.where(
        spot == WORDS, count, jnp.where(spot == WORDS + 1, most, 0.0)
    )

    for copy in [stage_x, stage_y, pair] + stage_t + stage_f:
        copy.wait_send()


def render_kernel(
    value_ref, order_ref, table_ref, taylor_table_ref, dirty_ref, fit_ref,
    residual_hbm, taylor_hbm,
    canvas, spill, canvas_t, spill_t, residual_ref, taylor_ref, amp_ref, list_ref, sems, out_sems,
):
    near = (value_ref.shape[0] + 1024) // 2
    ends = (pl.ds(0, near), pl.ds(near, value_ref.shape[0] - near))
    fetches = [
        pltpu.make_async_copy(value_ref.at[ends[0]], amp_ref.at[ends[0]], sems.at[0]),
        pltpu.make_async_copy(order_ref, list_ref, sems.at[1]),
        pltpu.make_async_copy(value_ref.at[ends[1]], amp_ref.at[ends[1]], sems.at[2]),
    ]
    for fetch in fetches:
        fetch.start()
    for block in range(BLOCKS - 1):
        for ref, used, first in (
            (canvas, block > 0, ROW_BASE), (spill, block < 4, ROW_BASE),
            (canvas_t, block > 0, ROW_BASE - HALF), (spill_t, block < 4, ROW_BASE - HALF),
        ):
            if used:
                rows = ROW_BASE + SIDE - first
                ref[pl.ds(block * CANVAS + first, rows), :] = jnp.zeros((rows, 128), jnp.float32)
    for fetch in fetches[:2]:
        fetch.wait()
    half_lane = lax.bitwise_and(lax.broadcasted_iota(jnp.int32, (HALF, 128), 1), 63)
    count = amp_ref[near - 1024 + WORDS].astype(jnp.int32)
    crowded = amp_ref[near - 1024 + WORDS + 1] > 4.0

    @pl.when(crowded)
    def _():
        fetches[2].wait()


    def step(first_of_all, group, index, carry):
        for g in range(group):
            slot = list_ref[first_of_all + index * group + g]
            packed = amp_ref[slot].astype(jnp.int32)
            amps = [amp_ref[slot + 4 + t] for t in range(TAYLOR)]
            first = lax.bitwise_and(packed, 2047)
            shift = lax.bitwise_and(lax.shift_right_logical(packed, 11), 63)
            base = lax.shift_right_logical(packed, 17) * HALF
            low = pl.multiple_of(base, HALF)
            high = pl.multiple_of(2 * base, PATCH)
            patch = fit = None
            for t in range(TAYLOR):
                term = amps[t] * table_ref[pl.ds(high + t * SCALES * PATCH, PATCH), :]
                patch = term if t == 0 else patch + term
                term = amps[t] * taylor_table_ref[pl.ds(low + t * SCALES * HALF, HALF), :]
                fit = term if t == 0 else fit + term
            patch = patch.astype(jnp.bfloat16).astype(jnp.float32)
            keep = half_lane >= shift
            other = jnp.logical_not(keep)
            sums = []
            for value, inside, beyond, at in (
                (patch[:HALF], canvas, spill, first),
                (patch[HALF:], canvas, spill, first + HALF),
                (fit, canvas_t, spill_t, first),
            ):
                value = pltpu.roll(value, shift, 1)
                for mask, target in ((keep, inside), (other, beyond)):
                    here = target.at[pl.ds(at, HALF), :]
                    sums.append((here, here[...] + value, mask))
            for here, value, mask in sums:
                pltpu.store(here, value, mask=mask)
        return carry

    done = 0
    for group in GROUPS:
        left = count - done + (group - 1 if group == GROUPS[-1] else 0)
        turns = left // group
        lax.fori_loop(0, turns, functools.partial(step, done, group), 0)
        done = done + turns * group

    @pl.when(jnp.logical_not(crowded))
    def _():
        fetches[2].wait()

    rows = OUT_ROWS
    lower = lax.broadcasted_iota(jnp.int32, (rows, 128), 1) < 64

    def mix(low, high):
        return jnp.where(lower, low, high)

    copies = []
    for r in range(0, SIDE, rows):
        for j in range(2):

            def at(ref, block, first):
                start = (block + 2 * j) * CANVAS + ROW_BASE + r + first
                return ref[pl.ds(start, rows), :]

            c1, c2 = at(canvas, 1, 0), at(canvas, 2, 0)
            s1, s2 = at(spill, 0, 0), at(spill, 1, 0)
            here = (slice(r, r + rows), slice(j * 128, j * 128 + 128))
            model = mix(c1, s2) + pltpu.roll(mix(c2, s1), 64, 1)
            residual_ref[(0,) + here] = dirty_ref[(0,) + here] - model
            model = mix(s1, c2) + pltpu.roll(mix(s2, c1), 64, 1)
            residual_ref[(1,) + here] = dirty_ref[(1,) + here] - model
            straight = mix(
                at(canvas_t, 1, 0) + at(spill_t, 0, -HALF), at(canvas_t, 2, -HALF) + at(spill_t, 1, 0)
            )
            crossed = mix(
                at(canvas_t, 2, 0) + at(spill_t, 1, -HALF), at(canvas_t, 1, -HALF) + at(spill_t, 0, 0)
            )
            taylor_ref[here] = fit_ref[here] - (straight + pltpu.roll(crossed, 64, 1))
        part = r // rows
        copies.append(
            pltpu.make_async_copy(
                residual_ref.at[:, pl.ds(r, rows), :], residual_hbm.at[:, pl.ds(r, rows), :],
                out_sems.at[0, part],
            )
        )
        copies.append(
            pltpu.make_async_copy(
                taylor_ref.at[pl.ds(r, rows), :], taylor_hbm.at[pl.ds(r, rows), :],
                out_sems.at[1, part],
            )
        )
        copies[-2].start()
        copies[-1].start()
    for copy in copies:
        copy.wait()


def per_device(dirty, psf, comp_tile, comp_offset, comp_scale, comp_amp, fit_weight):
    n_band, n_ty, n_tx = (lax.axis_size(a) for a in ("band", "ty", "tx"))
    sources, listed = n_ty * n_tx, comp_tile.shape[0]
    lists = max(1, sources * SLOTS // 128)
    vmem = pl.BlockSpec(memory_space=pltpu.VMEM)
    hbm = pl.BlockSpec(memory_space=pltpu.HBM)
    dma = pltpu.SemaphoreType.DMA
    f32, bf16 = jnp.float32, jnp.bfloat16
    value, order, table, taylor_table, fit = pl.pallas_call(
        functools.partial(exchange_kernel, n_band, n_ty, n_tx),
        out_shape=(
            jax.ShapeDtypeStruct((sources // 2 + 8, 128), f32),
            jax.ShapeDtypeStruct((lists, 128), jnp.int32),
            jax.ShapeDtypeStruct((PAD_K * PATCH, 128), f32),
            jax.ShapeDtypeStruct((PAD_K * HALF, 128), f32),
            jax.ShapeDtypeStruct((SIDE, SIDE), f32),
        ),
        in_specs=[hbm] * 7,
        out_specs=(vmem,) * 5,
        scratch_shapes=[
            pltpu.VMEM((1, listed), jnp.int32), pltpu.VMEM((2, listed), jnp.int32),
            pltpu.VMEM((1, listed), jnp.int32), pltpu.VMEM((TAYLOR, listed), f32),
            pltpu.SMEM((2, TAYLOR), f32), pltpu.VMEM((2, SIDE, SIDE), f32),
            pltpu.VMEM((ROWS_K, 2, 2 * WIDE), bf16),
            pltpu.VMEM((n_ty // 2, n_tx, 128), f32),
            pltpu.VMEM((n_ty, n_tx, 128), f32),
            pltpu.VMEM((n_ty, n_tx, 128), f32),
            pltpu.VMEM((2, PAD_K, 2 * WIDE), f32),
            pltpu.VMEM((n_band - 1, SIDE, SIDE), bf16),
            pltpu.VMEM((n_band - 1, SIDE, SIDE), bf16),
            pltpu.VMEM((n_band - 1, PAD_K, WIDE), f32),
            pltpu.VMEM((2, PAD_K, WIDE), f32),
            pltpu.VMEM((n_band - 1, PAD_K, WIDE), f32),
            dma((1,)), dma((1,)), dma((1,)), dma((1,)),
            dma((2, n_band - 1)), dma((2, n_band - 1)),
            dma((2,)), dma((1,)), dma((1,)), dma((7,)),
        ],
        compiler_params=pltpu.CompilerParams(
            collective_id=0, has_side_effects=True, vmem_limit_bytes=24 * 1024 * 1024
        ),
    )(
        *(
            pltpu.with_memory_space_constraint(operand, pltpu.HBM)
            for operand in (
                comp_tile.T, comp_offset.T, comp_scale[None, :], comp_amp.T, fit_weight, dirty,
                psf.transpose(1, 0, 2),
            )
        ),
    )
    residual, taylor = pl.pallas_call(
        render_kernel,
        out_shape=(
            jax.ShapeDtypeStruct((2, SIDE, SIDE), f32),
            jax.ShapeDtypeStruct((SIDE, SIDE), f32),
        ),
        in_specs=[vmem] * 6,
        out_specs=(hbm,) * 2,
        scratch_shapes=[
            pltpu.VMEM(((BLOCKS - 1) * CANVAS, 128), f32) for _ in range(4)
        ] + [
            pltpu.VMEM((2, SIDE, SIDE), f32), pltpu.VMEM((SIDE, SIDE), f32),
            pltpu.SMEM((value.size,), f32), pltpu.SMEM((order.size,), jnp.int32),
            dma((3,)), dma((2, SIDE // OUT_ROWS)),
        ],
        compiler_params=pltpu.CompilerParams(vmem_limit_bytes=24 * 1024 * 1024),
    )(
        value.reshape(-1), order.reshape(-1), table, taylor_table, dirty, fit,
    )
    return residual, taylor[None]


def solution(mesh):
    return jax.shard_map(
        per_device,
        mesh=mesh,
        in_specs=(
            P("band", "ty", "tx"),
            P("band", None, None),
            P(("ty", "tx"), None),
            P(("ty", "tx"), None),
            P(("ty", "tx")),
            P(("ty", "tx"), None),
            P("band", None),
        ),
        out_specs=(P("band", "ty", "tx"), P("band", "ty", "tx")),
        check_vma=False,
    )
```

profile of v0, /device:TPU:112, one launch (start us, length us, event | category | flops | bytes accessed | tf_op | source)
XLA Modules:
  0.0 32.1 jit_solution(13624499698611553620)
XLA Ops:
  0.6 0.0 copy-start
  0.6 24.1 %shard_map.86 = (f32[72,128]{1,0:T(8,128)S(1)}, s32[8,128]{1,0:T(8,128)S(1)}, f32[1152,128]{1,0:T(8,128)S(1)}, f32[576,128]{1,0:T(8,128)S(1)}, f32[256,256]{1,0:T(8,128)S(1)}) custom-call(s32[1,128]{1,0:T(1,128)} %bitcast.13, s32[2,128]{1,0:T(2,128)} %bitcast.12, s32[1,128]{1,0:T(1,128)} %bitcast.14, f32[4,128]{1,0:T(4,128)} %bitcast.11, f32[2,4]{1,0:T(2,128)} %weight_hbm.1, ...), custom_call_target="tpu_custom_call" | custom-call | tf_op jit(solution)/shard_map/pallas_call | solution.py:427
  24.7 0.0 copy-done
  24.7 7.3 %shard_map.87 = (f32[2,256,256]{2,1,0:T(8,128)}, f32[256,256]{1,0:T(8,128)}) custom-call(f32[9216]{0:T(1024)S(1)} %bitcast.8, s32[1024]{0:T(1024)S(1)} %bitcast.9, f32[1152,128]{1,0:T(8,128)S(1)} %get-tuple-element.11.table_ref, f32[576,128]{1,0:T(8,128)S(1)} %get-tuple-element.12.taylor_table_ref, f32[2,256,256]{2,1,0:T(8,128)S(1)} %copy-done, ...), custom_call_target="tpu_custom_call" | custom-call | tf_op jit(solution)/shard_map/pallas_call | solution.py:468
Async XLA Ops:
  0.6 24.1 %copy-start = (f32[2,256,256]{2,1,0:T(8,128)S(1)}, f32[2,256,256]{2,1,0:T(8,128)}, u32[]{:S(2)}) copy-start(f32[2,256,256]{2,1,0:T(8,128)} %dirty_ref.1) | copy-start | bytes 1572868
where the time goes:
time: 32 us; the launch traced here: 32.1 us
  Pallas kernels  31.4 us (98%)
  between operations  0.66 us (2%)
    pallas_call x1, Pallas kernels, per_device(): pl.pallas_call(functools.partial(exchange_kernel, n_band, n_ty, n_tx), ou...  24.1 us
    pallas_call x1, Pallas kernels, per_device(): pl.pallas_call(render_kernel, out_shape=(jax.ShapeDtypeStruct((2, SIDE, S...  7.33 us

commit v1 on v0

--- a/solution.py
+++ b/solution.py
@@ -166,7 +166,7 @@
     ]
     for o in range(1, n_band):
         w0, w1 = weight_ref[0, along_b[o - 1]], weight_ref[1, along_b[o - 1]]
-        tab_send[o - 1] = w0 * mine[0] + w1 * mine[1]
+        tab_send[o - 1] = (w0 * mine[0] + w1 * mine[1])[:ROWS_K]
         fit_send[o - 1] = (w0 * dirty_ref[0] + w1 * dirty_ref[1]).astype(jnp.bfloat16)
 
     w0, w1 = weight_ref[0, me_b], weight_ref[1, me_b]
@@ -214,7 +214,7 @@
     for copy in stage_t:
         copy.wait_recv()
     for o in range(n_band - 1):
-        tab_own[core] += tab_got[o]
+        tab_own[core, 0:ROWS_K] += tab_got[o]
     band_table(1)
     pair = pltpu.make_async_remote_copy(
         src_ref=tab_own.at[core], dst_ref=tab_own.at[core],
@@ -446,9 +446,9 @@
             pltpu.VMEM((2, PAD_K, 2 * WIDE), f32),
             pltpu.VMEM((n_band - 1, SIDE, SIDE), bf16),
             pltpu.VMEM((n_band - 1, SIDE, SIDE), bf16),
-            pltpu.VMEM((n_band - 1, PAD_K, WIDE), f32),
+            pltpu.VMEM((n_band - 1, ROWS_K, WIDE), f32),
             pltpu.VMEM((2, PAD_K, WIDE), f32),
-            pltpu.VMEM((n_band - 1, PAD_K, WIDE), f32),
+            pltpu.VMEM((n_band - 1, ROWS_K, WIDE), f32),
             dma((1,)), dma((1,)), dma((1,)), dma((1,)),
             dma((2, n_band - 1)), dma((2, n_band - 1)),
             dma((2,)), dma((1,)), dma((1,)), dma((7,)),

time: 32 us -> 32.2 us (level)
  the two profiles are of different devices: /device:TPU:112 before, /device:TPU:16 now
where the time goes in v1:
time: 32.2 us; the launch traced here: 32.3 us
  Pallas kernels  31.7 us (98%)
  between operations  0.66 us (2%)
    pallas_call x1, Pallas kernels, per_device(): pl.pallas_call(functools.partial(exchange_kernel, n_band, n_ty, n_tx), ou...  25 us
    pallas_call x1, Pallas kernels, per_device(): pl.pallas_call(render_kernel, out_shape=(jax.ShapeDtypeStruct((2, SIDE, S...  6.69 us

profile of v1, /device:TPU:16, one launch (start us, length us, event | category | flops | bytes accessed | tf_op | source)
XLA Modules:
  0.0 32.3 jit_solution(1502859143232214259)
XLA Ops:
  0.6 0.0 copy-start
  0.6 25.0 %shard_map.86 = (f32[72,128]{1,0:T(8,128)S(1)}, s32[8,128]{1,0:T(8,128)S(1)}, f32[1152,128]{1,0:T(8,128)S(1)}, f32[576,128]{1,0:T(8,128)S(1)}, f32[256,256]{1,0:T(8,128)S(1)}) custom-call(s32[1,128]{1,0:T(1,128)} %bitcast.13, s32[2,128]{1,0:T(2,128)} %bitcast.12, s32[1,128]{1,0:T(1,128)} %bitcast.14, f32[4,128]{1,0:T(4,128)} %bitcast.11, f32[2,4]{1,0:T(2,128)} %weight_hbm.1, ...), custom_call_target="tpu_custom_call" | custom-call | tf_op jit(solution)/shard_map/pallas_call | solution.py:427
  25.6 0.0 copy-done
  25.6 6.7 %shard_map.87 = (f32[2,256,256]{2,1,0:T(8,128)}, f32[256,256]{1,0:T(8,128)}) custom-call(f32[9216]{0:T(1024)S(1)} %bitcast.8, s32[1024]{0:T(1024)S(1)} %bitcast.9, f32[1152,128]{1,0:T(8,128)S(1)} %get-tuple-element.11.table_ref, f32[576,128]{1,0:T(8,128)S(1)} %get-tuple-element.12.taylor_table_ref, f32[2,256,256]{2,1,0:T(8,128)S(1)} %copy-done, ...), custom_call_target="tpu_custom_call" | custom-call | tf_op jit(solution)/shard_map/pallas_call | solution.py:468
Async XLA Ops:
  0.6 25.0 %copy-start = (f32[2,256,256]{2,1,0:T(8,128)S(1)}, f32[2,256,256]{2,1,0:T(8,128)}, u32[]{:S(2)}) copy-start(f32[2,256,256]{2,1,0:T(8,128)} %dirty_ref.1) | copy-start | bytes 1572868

commit v2 on v1

--- a/solution.py
+++ b/solution.py
@@ -110,12 +110,15 @@
 ):
     me_b, me_y, me_x = lax.axis_index("band"), lax.axis_index("ty"), lax.axis_index("tx")
     barrier = pltpu.get_barrier_semaphore()
-    along_x = [lax.rem(me_x + o, n_tx) for o in range(1, n_tx)]
-    along_y = [lax.rem(me_y + o, n_ty) for o in range(1, n_ty)]
+    def far_first(count):
+        return sorted(range(1, count), key=lambda o: -min(o, count - o))
+
+    along_x = [lax.rem(me_x + o, n_tx) for o in far_first(n_tx)]
+    along_y = [lax.rem(me_y + o, n_ty) for o in far_first(n_ty)]
     along_b = [lax.rem(me_b + o, n_band) for o in range(1, n_band)]
     partners = (
-        [(me_b, me_y, x) for x in along_x]
-        + [(me_b, y, me_x) for y in along_y]
+        [(me_b, y, me_x) for y in along_y]
+        + [(me_b, me_y, x) for x in along_x]
         + [(b, me_y, me_x) for b in along_b]
     )
     for partner in partners:
@@ -152,7 +155,7 @@
             device_id=(me_b, y, me_x), device_id_type=MESH,
         )
         copy.start()
-    stage_y = in_all(cross.at[pl.ds(0, n_ty - 1)], y_send, y_recv, partners[-n_band])
+    stage_y = in_all(cross.at[pl.ds(0, n_ty - 1)], y_send, y_recv, partners[0])
     own = pltpu.make_async_copy(send.at[me_y // 2], cross.at[me_y], own_sem.at[0])
     own.start()
     for load in loads[4:]:
@@ -207,7 +210,7 @@
             device_id=(me_b, me_y, x), device_id_type=MESH,
         )
         copy.start()
-    stage_x = in_all(got.at[:, pl.ds(0, n_tx - 1), :], x_send, x_recv, partners[0])
+    stage_x = in_all(got.at[:, pl.ds(0, n_tx - 1), :], x_send, x_recv, partners[-n_band])
     own = pltpu.make_async_copy(cross.at[:, me_x, :], got.at[:, me_x, :], own_sem.at[1])
     own.start()
 

time: 32.2 us -> 32.7 us (1.016)
  the two profiles are of different devices: /device:TPU:16 before, /device:TPU:8 now
where the time goes in v2:
time: 32.7 us; the launch traced here: 32.5 us
  Pallas kernels  31.9 us (98%)
  between operations  0.66 us (2%)
    pallas_call x1, Pallas kernels, per_device(): pl.pallas_call(functools.partial(exchange_kernel, n_band, n_ty, n_tx), ou...  25.2 us
    pallas_call x1, Pallas kernels, per_device(): pl.pallas_call(render_kernel, out_shape=(jax.ShapeDtypeStruct((2, SIDE, S...  6.68 us

profile of v2, /device:TPU:8, one launch (start us, length us, event | category | flops | bytes accessed | tf_op | source)
XLA Modules:
  0.0 32.5 jit_solution(6820126340012019335)
XLA Ops:
  0.6 0.0 copy-start
  0.6 25.2 %shard_map.86 = (f32[72,128]{1,0:T(8,128)S(1)}, s32[8,128]{1,0:T(8,128)S(1)}, f32[1152,128]{1,0:T(8,128)S(1)}, f32[576,128]{1,0:T(8,128)S(1)}, f32[256,256]{1,0:T(8,128)S(1)}) custom-call(s32[1,128]{1,0:T(1,128)} %bitcast.13, s32[2,128]{1,0:T(2,128)} %bitcast.12, s32[1,128]{1,0:T(1,128)} %bitcast.14, f32[4,128]{1,0:T(4,128)} %bitcast.11, f32[2,4]{1,0:T(2,128)} %weight_hbm.1, ...), custom_call_target="tpu_custom_call" | custom-call | tf_op jit(solution)/shard_map/pallas_call | solution.py:430
  25.8 0.0 copy-done
  25.8 6.7 %shard_map.87 = (f32[2,256,256]{2,1,0:T(8,128)}, f32[256,256]{1,0:T(8,128)}) custom-call(f32[9216]{0:T(1024)S(1)} %bitcast.8, s32[1024]{0:T(1024)S(1)} %bitcast.9, f32[1152,128]{1,0:T(8,128)S(1)} %get-tuple-element.11.table_ref, f32[576,128]{1,0:T(8,128)S(1)} %get-tuple-element.12.taylor_table_ref, f32[2,256,256]{2,1,0:T(8,128)S(1)} %copy-done, ...), custom_call_target="tpu_custom_call" | custom-call | tf_op jit(solution)/shard_map/pallas_call | solution.py:471
Async XLA Ops:
  0.6 25.2 %copy-start = (f32[2,256,256]{2,1,0:T(8,128)S(1)}, f32[2,256,256]{2,1,0:T(8,128)}, u32[]{:S(2)}) copy-start(f32[2,256,256]{2,1,0:T(8,128)} %dirty_ref.1) | copy-start | bytes 1572868

commit v3 on v0

--- a/solution.py
+++ b/solution.py
@@ -21,7 +21,7 @@
 COL_BASE = 64
 BLOCKS = 6
 CANVAS = 352
-GROUPS = (48, 16, 8)
+GROUPS = (64, 16, 8)
 OUT_ROWS = 64
 MESH = pl.DeviceIdType.MESH
 

time: 32 us -> 32.2 us (level)
  the two profiles are of different devices: /device:TPU:112 before, /device:TPU:8 now
where the time goes in v3:
time: 32.2 us; the launch traced here: 32.1 us
  Pallas kernels  31.5 us (98%)
  between operations  0.66 us (2%)
    pallas_call x1, Pallas kernels, per_device(): pl.pallas_call(functools.partial(exchange_kernel, n_band, n_ty, n_tx), ou...  25 us
    pallas_call x1, Pallas kernels, per_device(): pl.pallas_call(render_kernel, out_shape=(jax.ShapeDtypeStruct((2, SIDE, S...  6.48 us

profile of v3, /device:TPU:8, one launch (start us, length us, event | category | flops | bytes accessed | tf_op | source)
XLA Modules:
  0.0 32.1 jit_solution(11154227598118452523)
XLA Ops:
  0.6 0.0 copy-start
  0.6 25.0 %shard_map.86 = (f32[72,128]{1,0:T(8,128)S(1)}, s32[8,128]{1,0:T(8,128)S(1)}, f32[1152,128]{1,0:T(8,128)S(1)}, f32[576,128]{1,0:T(8,128)S(1)}, f32[256,256]{1,0:T(8,128)S(1)}) custom-call(s32[1,128]{1,0:T(1,128)} %bitcast.13, s32[2,128]{1,0:T(2,128)} %bitcast.12, s32[1,128]{1,0:T(1,128)} %bitcast.14, f32[4,128]{1,0:T(4,128)} %bitcast.11, f32[2,4]{1,0:T(2,128)} %weight_hbm.1, ...), custom_call_target="tpu_custom_call" | custom-call | tf_op jit(solution)/shard_map/pallas_call | solution.py:427
  25.6 0.0 copy-done
  25.6 6.5 %shard_map.87 = (f32[2,256,256]{2,1,0:T(8,128)}, f32[256,256]{1,0:T(8,128)}) custom-call(f32[9216]{0:T(1024)S(1)} %bitcast.8, s32[1024]{0:T(1024)S(1)} %bitcast.9, f32[1152,128]{1,0:T(8,128)S(1)} %get-tuple-element.11.table_ref, f32[576,128]{1,0:T(8,128)S(1)} %get-tuple-element.12.taylor_table_ref, f32[2,256,256]{2,1,0:T(8,128)S(1)} %copy-done, ...), custom_call_target="tpu_custom_call" | custom-call | tf_op jit(solution)/shard_map/pallas_call | solution.py:468
Async XLA Ops:
  0.6 25.0 %copy-start = (f32[2,256,256]{2,1,0:T(8,128)S(1)}, f32[2,256,256]{2,1,0:T(8,128)}, u32[]{:S(2)}) copy-start(f32[2,256,256]{2,1,0:T(8,128)} %dirty_ref.1) | copy-start | bytes 1572868
